TPU v7x, 32 devices: a whole 2x2x4 slice. The times are simulated.
32 devices in a mesh: replica: 4 (over y, core), shard: 8 (over z, x).
Axes of the slice: x: 2, y: 2, z: 4, core: 2. Of those that a mesh axis runs over, the one named last changes fastest.
Arguments:
- tokens: bfloat16 [4, 1024, 3072], P('replica', 'shard'), may hold values from -6 to 6
- weight_slots: bfloat16 [4, 576, 128, 128], P('replica', 'shard'), may hold values from -0.15625 to 0.15625
- block_rows: int32 [96, 12], replicated, may hold values from 0 to 23, as said below
- block_owner: int32 [96, 12], replicated, may hold values from 0 to 7, as said below
- block_slot: int32 [96, 12], replicated, may hold values from 0 to 71, as said below
- grad_act: bfloat16 [4, 1024, 12288], P(None, 'shard', 'replica'), may hold values from -6 to 6
Outputs:
- act_out: bfloat16 [4, 1024, 12288], P(None, 'shard', 'replica')
- grad_tokens: bfloat16 [4, 1024, 3072], P('replica', 'shard')
- grad_slots: float32 [4, 576, 128, 128], P('replica', 'shard')
Inputs may be any that keep to these rules, and one draw needn't show every extreme that they name: `block_rows`: each row holds 12 distinct increasing block rows; within each group of 24 consecutive block columns every block row appears in exactly 12 of them. `block_owner`: within each group of 24 consecutive block columns no owner holds more than 72 blocks, and in every group some owner holds exactly 72. `block_slot`: within each group of 24 consecutive block columns the pairs of owner and slot are distinct.
All inputs are finite; a program needn't handle non-finite values.
Results may differ from a plain program's by a relative error of at most 0.01.
Values may be sent and summed in bfloat16 or wider, within the bound.
A program may use at most 192 MiB of HBM per device.

v0:
```python
import math

import jax
import jax.numpy as jnp
from jax import lax
from jax.sharding import PartitionSpec as P


def gelu_value(hidden):
    return 0.5 * hidden * (1.0 + lax.erf(hidden * 0.7071067811865476))


def gelu_slope(hidden):
    normal_cdf = 0.5 * (1.0 + lax.erf(hidden * 0.7071067811865476))
    return normal_cdf + hidden * jnp.exp(-0.5 * hidden * hidden) * 0.3989422804014327


def local(tokens, weight_slots, block_rows, block_owner, block_slot, grad_act):
    replica_count = lax.axis_size("replica")
    shard_count = lax.axis_size("shard")
    replica_index = lax.axis_index("replica")
    block_size = weight_slots.shape[3]
    capacity = weight_slots.shape[1]
    tok_rows = tokens.shape[1]
    model_width = tokens.shape[2]
    row_blocks = model_width // block_size
    keep_count = block_rows.shape[1]
    slice_cols = grad_act.shape[2] // block_size
    all_rows = replica_count * tok_rows
    own_slots = weight_slots.reshape(capacity, block_size, block_size)
    start_col = replica_index * slice_cols
    rows_here = lax.dynamic_slice_in_dim(block_rows, start_col, slice_cols, 0)
    owner_here = lax.dynamic_slice_in_dim(block_owner, start_col, slice_cols, 0)
    slot_here = lax.dynamic_slice_in_dim(block_slot, start_col, slice_cols, 0)
    place_here = owner_here * capacity + slot_here
    owner_slab = lax.all_gather(own_slots, "shard", axis=0, tiled=True)
    weight_cols = jnp.take(owner_slab, place_here.reshape(-1), axis=0)
    weight_cols = weight_cols.reshape(slice_cols, keep_count * block_size, block_size)
    gathered = lax.all_gather(tokens, "replica", axis=0, tiled=True)
    token_blocks = gathered.reshape(all_rows, row_blocks, block_size)
    cot_cols = jnp.transpose(grad_act.reshape(all_rows, slice_cols, block_size), (1, 0, 2))

    def column_step(grad_rows, inputs):
        rows_col, weight_col, cot_col = inputs
        col_inputs = jnp.take(token_blocks, rows_col, axis=1).reshape(
            all_rows, keep_count * block_size
        )
        hidden = jnp.dot(col_inputs, weight_col, preferred_element_type=jnp.float32)
        act_col = gelu_value(hidden).astype(jnp.bfloat16)
        slope = (cot_col.astype(jnp.float32) * gelu_slope(hidden)).astype(jnp.bfloat16)
        block_grad = lax.dot_general(
            col_inputs, slope, (((0,), (0,)), ((), ())), preferred_element_type=jnp.float32
        )
        back = lax.dot_general(
            slope, weight_col, (((1,), (1,)), ((), ())), preferred_element_type=jnp.float32
        )
        grad_rows = grad_rows.at[:, rows_col].add(back.reshape(all_rows, keep_count, block_size))
        return (grad_rows, (act_col, block_grad))

    start_rows = jnp.zeros((all_rows, row_blocks, block_size), jnp.float32)
    grad_rows, (act_cols, grad_blocks) = lax.scan(
        column_step, start_rows, (rows_here, weight_cols, cot_cols)
    )
    partial_grad = grad_rows.reshape(replica_count, tok_rows, model_width)
    grad_tokens = lax.psum_scatter(
        partial_grad.astype(jnp.bfloat16), "replica", scatter_dimension=0, tiled=True
    )
    grad_scale = 1.0 / math.sqrt(replica_count * shard_count * tok_rows)
    total_blocks = slice_cols * keep_count
    grad_flat = grad_blocks.reshape(total_blocks, block_size, block_size)
    slot_grid = jnp.zeros((shard_count * capacity, block_size, block_size), jnp.float32)
    slot_grid = slot_grid.at[place_here.reshape(-1)].set(grad_flat)
    summed = lax.psum_scatter(
        slot_grid.astype(jnp.bfloat16), "shard", scatter_dimension=0, tiled=True
    ).astype(jnp.float32)
    grad_slots = (summed * grad_scale).reshape(1, capacity, block_size, block_size)
    act_out = jnp.transpose(act_cols, (1, 0, 2)).reshape(
        replica_count, tok_rows, slice_cols * block_size
    )
    return (act_out, grad_tokens, grad_slots)


def solution(mesh):
    return jax.shard_map(
        local,
        mesh=mesh,
        in_specs=(
            P("replica", "shard", None),
            P("replica", "shard", None, None),
            P(),
            P(),
            P(),
            P(None, "shard", "replica"),
        ),
        out_specs=(
            P(None, "shard", "replica"),
            P("replica", "shard", None),
            P("replica", "shard", None, None),
        ),
        check_vma=False,
    )
```

profile of v0, /device:TPU:0, one launch (start us, length us, event | category | flops | bytes accessed | tf_op | source)
XLA Modules:
  0.0 1458.7 jit_solution(657302423886190313)
XLA Ops:
  13.4 27.5 %all-gather.4.cloned.1.call-done = bf16[4,128,3072]{2,1,0:T(8,128)(2,1)} async-done(((bf16[1,128,3072]{2,1,0:T(8,128)(2,1)}), bf16[4,128,3072]{2,1,0:T(8,128)(2,1)}) %all-gather.4.cloned.1.call-update) | async-done | bytes 3145744 | tf_op jit(solution)/shard_map/all_gather | solution.py:39
  46.1 358.8 %all-gather.6.cloned.1.call-done = bf16[1,576,128,128]{3,2,0,1:T(8,128)(2,1)} async-done(((bf16[1,72,128,128]{3,2,0,1:T(8,128)(2,1)}), bf16[1,576,128,128]{3,2,0,1:T(8,128)(2,1)}) %all-gather.6.cloned.1.call-update) | async-done | bytes 18874384 | tf_op jit(solution)/shard_map/all_gather | solution.py:36
  404.9 16.8 %gather_fusion.1 = bf16[288,128,128]{2,1,0:T(8,128)(2,1)} fusion(bf16[576,128,128]{2,1,0:T(8,128)(2,1)} %bitcast.109, s32[1024]{0:T(1024)S(1)} %pad_clamp_fusion.1), kind=kCustom, calls=%fused_computation.1 | custom fusion | bytes 18875520 | tf_op jit(solution)/shard_map/jit(_take)/gather | solution.py:37
  421.7 10.4 bitcast_select_fusion.1
  435.4 577.2 %while.14 = (s32[]{:T(128)}, f32[512,24,128]{2,0,1:T(8,128)}, bf16[24,512,128]{2,1,0:T(8,128)(2,1)}, f32[24,1536,128]{2,1,0:T(8,128)}, s32[24,12]{1,0:T(8,128)},...) while((s32[]{:T(128)}, f32[512,24,128]{2,0,1:T(8,128)}, ...), condition=%wide.region_2.3_spmd, body=%wide.region_0.0_spmd.sunk | while | flops 608109696 | bytes 43393552 | solution.py:61
  448.4 8.0 scatter_fusion
  496.3 8.1 scatter_fusion
  520.3 8.1 scatter_fusion
  544.3 8.1 scatter_fusion
  568.4 8.2 scatter_fusion
  592.5 8.1 scatter_fusion
  616.6 8.2 scatter_fusion
  640.8 8.2 scatter_fusion
  664.9 8.1 scatter_fusion
  688.9 8.0 scatter_fusion
  712.9 8.1 scatter_fusion
  736.9 8.2 scatter_fusion
  761.0 8.2 scatter_fusion
  785.1 8.1 scatter_fusion
  809.2 8.1 scatter_fusion
  833.2 8.1 scatter_fusion
  857.2 8.2 scatter_fusion
  881.3 8.2 scatter_fusion
  929.3 8.1 scatter_fusion
  953.4 8.1 scatter_fusion
  977.4 8.1 scatter_fusion
  1001.5 8.2 scatter_fusion
  1012.6 12.6 broadcast_in_dim.61
  1025.2 52.0 %scatter_fusion.1 = f32[576,128,128]{2,1,0:T(8,128)} fusion(f32[576,128,128]{2,1,0:T(8,128)} %broadcast_in_dim.61, s32[288]{0:T(512)S(1)} %copy-done.7, f32[288,128,128]{2,1,0:T(8,128)} %bitcast.106), kind=kCustom, calls=%fused_computation.3 | custom fusion | bytes 56624256 | tf_op jit(solution)/shard_map/scatter | solution.py:72
  1077.2 20.9 %convert_element_type.26 = bf16[576,128,128]{2,1,0:T(8,128)(2,1)} convert(f32[576,128,128]{2,1,0:T(8,128)} %scatter_fusion.1) | non-fusion elementwise | flops 9437184 | bytes 56623104 | tf_op jit(solution)/shard_map/convert_element_type | solution.py:74
  1113.4 298.6 %reduce-scatter.5.cloned.1.call-done = bf16[72,128,128]{2,1,0:T(8,128)(2,1)} async-done(((bf16[576,128,128]{2,1,0:T(8,128)(2,1)}), bf16[72,128,128]{2,1,0:T(8,128)(2,1)}) %reduce-scatter.5.cloned.1.call-update) | async-done | bytes 2359312 | tf_op jit(solution)/shard_map/reduce_scatter | solution.py:73
  1416.5 35.6 %reduce-scatter.3.cloned.1.call-done = bf16[1,128,3072]{2,1,0:T(8,128)(2,1)} async-done(((bf16[4,128,3072]{2,1,0:T(8,128)(2,1)}), bf16[1,128,3072]{2,1,0:T(8,128)(2,1)}) %reduce-scatter.3.cloned.1.call-update) | async-done | bytes 786448 | tf_op jit(solution)/shard_map/reduce_scatter | solution.py:65
  (503 shorter events, 431.5 us)
Async XLA Ops:
  7.2 2.9 copy-start.5
  7.2 33.7 %all-gather.4.cloned.1.call-start = ((), (), s32[]{:S(2)}) async-start(), calls=%async_computation.2 | async-start | bytes 3932160 | tf_op jit(solution)/shard_map/all_gather | solution.py:39
  7.9 397.0 %all-gather.6.cloned.1.call-start = ((), (), s32[]{:S(2)}) async-start(), calls=%async_computation.5 | async-start | bytes 21233664 | tf_op jit(solution)/shard_map/all_gather | solution.py:36
  8.7 1403.3 %reduce-scatter.5.cloned.1.call-start = ((), (), s32[]{:S(2)}) async-start(), calls=%async_computation.4 | async-start | bytes 21233664 | tf_op jit(solution)/shard_map/reduce_scatter | solution.py:73
  13.3 30.3 %copy-start.6 = (s32[288]{0:T(512)}, s32[288]{0:T(512)S(1)}, u32[]{:S(2)}) copy-start(s32[288]{0:T(512)S(1)} %fusion.15) | copy-start | bytes 3460
  448.4 8.1 copy-start.4
  472.3 8.0 copy-start.4
  496.3 8.1 copy-start.4
  520.3 8.1 copy-start.4
  544.3 8.2 copy-start.4
  568.4 8.2 copy-start.4
  592.5 8.2 copy-start.4
  616.6 8.2 copy-start.4
  640.8 8.2 copy-start.4
  664.9 8.1 copy-start.4
  688.9 8.1 copy-start.4
  712.9 8.1 copy-start.4
  736.9 8.2 copy-start.4
  761.0 8.2 copy-start.4
  785.1 8.1 copy-start.4
  809.2 8.1 copy-start.4
  833.1 8.2 copy-start.4
  857.2 8.2 copy-start.4
  881.3 8.2 copy-start.4
  905.4 8.0 copy-start.4
  929.3 8.2 copy-start.4
  953.4 8.1 copy-start.4
  977.4 8.1 copy-start.4
  1001.5 8.2 copy-start.4
  1012.6 12.6 copy-start.7
  1098.1 354.0 %reduce-scatter.3.cloned.1.call-start = ((), (), s32[]{:S(2)}) async-start(), calls=%async_computation.3 | async-start | bytes 3932160 | tf_op jit(solution)/shard_map/reduce_scatter | solution.py:65
  1110.6 341.6 %copy-start.1 = (s32[96,12]{0,1:T(8,128)S(1)}, s32[96,12]{0,1:T(8,128)}, u32[]{:S(2)}) copy-start(s32[96,12]{0,1:T(8,128)} %param.10) | copy-start | bytes 13828
  (51 other events, 64.9 us)
Sparse Core Ops, SparseCore 0:
  9.6 31.2 all-gather.3
  42.4 362.4 all-gather.5
  1098.2 313.7 reduce-scatter.4
  1415.0 37.1 reduce-scatter.2
where the time goes:
time: 1470 us; the launch traced here: 1460 us
  waiting for transfers between devices  722 us (49%)
  other arithmetic  308 us (21%)
  local copies, waits for them, and re-layouts  276 us (19%)
  matrix products  137 us (9%)
    all_gather x1, waiting for transfers between devices, local(): owner_slab = lax.all_gather(own_slots, 'shard', axis=0, tiled=True)  359 us
    reduce_scatter x1, waiting for transfers between devices, local(): lax.psum_scatter(slot_grid.astype(jnp.bfloat16), 'shard', scatter_dimensi...  299 us
    scatter-add x24, other arithmetic, column_step(): grad_rows.at[:, rows_col]  195 us
    gather x48, local copies, waits for them, and re-layouts, column_step(): jnp.take(token_blocks, rows_col, axis=1)  82.4 us
    dot_general x24, matrix products, column_step(): lax.dot_general(col_inputs, slope, (((0,), (0,)), ((), ())), preferred_el...  71.1 us
    scatter x1, local copies, waits for them, and re-layouts, local(): slot_grid = slot_grid.at[place_here.reshape(-1)].set(grad_flat)  52 us
    select_n x48, other arithmetic, column_step(): jnp.take(token_blocks, rows_col, axis=1)  40.8 us
    select_n x24, local copies, waits for them, and re-layouts, column_step(): jnp.take(token_blocks, rows_col, axis=1)  38.5 us
  transfers between devices with their start and end apart: 4, of which 4 were waited for; matrix products, arithmetic and copies ran while one was open for 2% of the time, Pallas kernels for 0%

commit v1 on v0

v1 whole, which is shorter than its diff:
```python
import functools
import math

import jax
import jax.numpy as jnp
from jax import lax
from jax.experimental import pallas as pl
from jax.experimental.pallas import tpu as pltpu
from jax.sharding import PartitionSpec as P

GROUP = 4
PIECES = 6
MIB = 1 << 20


def gelu_both(hidden):
    cdf = 0.5 * (1.0 + lax.erf(hidden * 0.7071067811865476))
    slope = cdf + hidden * jnp.exp(-0.5 * hidden * hidden) * 0.3989422804014327
    return hidden * cdf, slope


def load_columns(step, slot, keep, idx_ref, rows_ref, slab_ref, wbuf, wsem):
    block = slab_ref.shape[1]
    wbuf[slot] = jnp.zeros(wbuf.shape[1:], wbuf.dtype)
    for col in range(GROUP):

        def body(j, carry, col=col):
            at = (step * GROUP + col) * keep + j
            row = pl.multiple_of(rows_ref[at] * block, block)
            pltpu.make_async_copy(
                slab_ref.at[idx_ref[at]],
                wbuf.at[slot, pl.ds(row, block), pl.ds(col * block, block)],
                wsem.at[slot],
            ).start()
            return carry

        lax.fori_loop(0, keep, body, 0)


def wait_columns(slot, keep, block, wbuf, wsem):
    part = wbuf.at[slot, pl.ds(0, keep * block), :]
    pltpu.make_async_copy(part, part, wsem.at[slot]).wait()


def forward_kernel(keep, idx_ref, rows_ref, pos_ref, tok_ref, tokt_ref, cot_ref, slab_ref,
                   act_ref, slope_ref, grads_ref, wbuf, gbuf, wsem, gsem):
    step = pl.program_id(0)
    steps = pl.num_programs(0)
    slot = lax.rem(step, 2)
    block = slab_ref.shape[1]
    rows = tok_ref.shape[0]
    width = tok_ref.shape[1]
    load = functools.partial(load_columns, keep=keep, idx_ref=idx_ref, rows_ref=rows_ref,
                             slab_ref=slab_ref, wbuf=wbuf, wsem=wsem)

    @pl.when(step == 0)
    def _():
        load(step, 0)

    @pl.when(step + 1 < steps)
    def _():
        load(step + 1, 1 - slot)

    wait_columns(slot, keep, block, wbuf, wsem)
    per = cot_ref.shape[1]

    def fwd(r, carry):
        at = pl.ds(pl.multiple_of(r * per, per), per)
        hidden = jnp.dot(tok_ref[at, :], wbuf[slot], preferred_element_type=jnp.float32)
        act, slope = gelu_both(hidden)
        act_ref[r] = act.astype(act_ref.dtype)
        slope = cot_ref[r].astype(jnp.float32) * slope
        slope_ref[at, :] = slope.astype(slope_ref.dtype)
        return carry

    lax.fori_loop(0, cot_ref.shape[0], fwd, 0)

    def drain(which):
        part = gbuf.at[which, pl.ds(0, keep * block), :]
        pltpu.make_async_copy(part, part, gsem.at[which]).wait()

    @pl.when(step >= 2)
    def _():
        drain(slot)

    tile = 512

    def back(m, carry):
        at = pl.ds(pl.multiple_of(m * tile, tile), tile)
        gbuf[slot, at, :] = jnp.dot(
            tokt_ref[at, :], slope_ref[...], preferred_element_type=jnp.float32
        ).astype(gbuf.dtype)
        return carry

    lax.fori_loop(0, width // tile, back, 0)

    for col in range(GROUP):

        def put(j, carry, col=col):
            at = (step * GROUP + col) * keep + j
            row = pl.multiple_of(rows_ref[at] * block, block)
            pltpu.make_async_copy(
                gbuf.at[slot, pl.ds(row, block), pl.ds(col * block, block)],
                grads_ref.at[pos_ref[at]],
                gsem.at[slot],
            ).start()
            return carry

        lax.fori_loop(0, keep, put, 0)

    @pl.when(step == steps - 1)
    def _():
        drain(slot)

        @pl.when(steps > 1)
        def _():
            drain(1 - slot)


def input_grad_kernel(keep, idx_ref, rows_ref, slope_ref, slab_ref, out_ref, wbuf, total, wsem):
    step = pl.program_id(0)
    steps = pl.num_programs(0)
    slot = lax.rem(step, 2)
    block = slab_ref.shape[1]
    load = functools.partial(load_columns, keep=keep, idx_ref=idx_ref, rows_ref=rows_ref,
                             slab_ref=slab_ref, wbuf=wbuf, wsem=wsem)

    @pl.when(step == 0)
    def _():
        load(step, 0)
        total[...] = jnp.zeros_like(total)

    @pl.when(step + 1 < steps)
    def _():
        load(step + 1, 1 - slot)

    wait_columns(slot, keep, block, wbuf, wsem)
    tile = 512

    def body(n, carry):
        at = pl.ds(pl.multiple_of(n * tile, tile), tile)
        total[:, at] += lax.dot_general(
            slope_ref[...], wbuf[slot, at, :], (((1,), (1,)), ((), ())),
            preferred_element_type=jnp.float32,
        )
        return carry

    lax.fori_loop(0, total.shape[1] // tile, body, 0)

    @pl.when(step == steps - 1)
    def _():
        out_ref[...] = total[...].astype(out_ref.dtype)


def gather_blocks(mine, shard_count):
    return lax.all_gather(mine, "shard", axis=0, tiled=False)


def reduce_blocks(grads, shard_count):
    return lax.psum_scatter(grads, "shard", scatter_dimension=0, tiled=False)


def exchange(send):
    return lax.all_to_all(send, "shard", 0, 0, tiled=True)


def local(tokens, weight_slots, block_rows, block_owner, block_slot, grad_act):
    replicas = lax.axis_size("replica")
    shards = lax.axis_size("shard")
    replica = lax.axis_index("replica")
    me = lax.axis_index("shard")
    block = weight_slots.shape[3]
    cap = weight_slots.shape[1]
    tok_rows, width = tokens.shape[1], tokens.shape[2]
    keep = block_rows.shape[1]
    slice_cols = grad_act.shape[2] // block
    all_rows = replicas * tok_rows
    count = slice_cols * keep
    per_pair = -(-cap // shards)
    per_dev = -(-count // (shards * PIECES)) * PIECES
    own_slots = weight_slots.reshape(cap, block, block)

    start_col = replica * slice_cols
    rows = lax.dynamic_slice_in_dim(block_rows, start_col, slice_cols, 0).reshape(-1)
    place = (lax.dynamic_slice_in_dim(block_owner, start_col, slice_cols, 0) * cap
             + lax.dynamic_slice_in_dim(block_slot, start_col, slice_cols, 0)).reshape(-1)
    rank = jnp.sum((place[None, :] < place[:, None]).astype(jnp.int32), axis=1)
    where_at = (rank % shards) * per_dev + rank // shards
    ranks = jnp.arange(count, dtype=jnp.int32)
    by_rank = jnp.sum(jnp.where(rank[None, :] == ranks[:, None], place[None, :], 0), axis=1)
    owners = jnp.arange(shards, dtype=jnp.int32)
    first = jnp.sum((place[None, :] < owners[:, None] * cap).astype(jnp.int32), axis=1)

    turn = jnp.arange(per_pair, dtype=jnp.int32)[None, :]
    my_first = first[me]
    send_rank = my_first + (owners[:, None] - my_first) % shards + turn * shards
    send_slot = jnp.clip(jnp.take(by_rank, jnp.clip(send_rank, 0, count - 1)) - me * cap, 0, cap - 1)
    hold_rank = jnp.clip(jnp.arange(per_dev, dtype=jnp.int32) * shards + me, 0, count - 1)
    hold_owner = jnp.take(by_rank, hold_rank) // cap
    hold_first = jnp.take(first, hold_owner)
    hold_from = hold_owner * per_pair + (hold_rank - hold_first) // shards
    back_rank = first[:, None] + (me - first[:, None]) % shards + turn * shards
    back_from = jnp.clip((back_rank - me) // shards, 0, per_dev - 1)
    slots = me * cap + jnp.arange(cap, dtype=jnp.int32)
    slot_rank = jnp.sum((place[None, :] < slots[:, None]).astype(jnp.int32), axis=1)
    slot_used = jnp.any(place[None, :] == slots[:, None], axis=1)
    slot_from = jnp.clip((slot_rank % shards) * per_pair + (slot_rank - my_first) // shards,
                         0, shards * per_pair - 1)

    gathered = lax.all_gather(tokens, "replica", axis=0, tiled=True).reshape(all_rows, width)
    sent = jnp.take(own_slots, send_slot.reshape(-1), axis=0)
    got = exchange(sent)
    held = jnp.take(got, hold_from, axis=0)
    slab = gather_blocks(held, shards).reshape(shards * per_dev, block, block)
    tok_t = gathered.T

    cols = GROUP * block
    act_out, slope, grads = pl.pallas_call(
        functools.partial(forward_kernel, keep),
        name="forward_and_weight_grad",
        out_shape=(
            jax.ShapeDtypeStruct((replicas, tok_rows, slice_cols * block), jnp.bfloat16),
            jax.ShapeDtypeStruct((all_rows, slice_cols * block), jnp.bfloat16),
            jax.ShapeDtypeStruct((shards * per_dev, block, block), jnp.bfloat16),
        ),
        grid_spec=pltpu.PrefetchScalarGridSpec(
            num_scalar_prefetch=3,
            grid=(slice_cols // GROUP,),
            in_specs=[
                pl.BlockSpec((all_rows, width), lambda i, *_: (0, 0)),
                pl.BlockSpec((width, all_rows), lambda i, *_: (0, 0)),
                pl.BlockSpec((replicas, tok_rows, cols), lambda i, *_: (0, 0, i)),
                pl.BlockSpec(memory_space=pl.ANY),
            ],
            out_specs=(
                pl.BlockSpec((replicas, tok_rows, cols), lambda i, *_: (0, 0, i)),
                pl.BlockSpec((all_rows, cols), lambda i, *_: (0, i)),
                pl.BlockSpec(memory_space=pl.ANY),
            ),
            scratch_shapes=[
                pltpu.VMEM((2, width, cols), jnp.bfloat16),
                pltpu.VMEM((2, width, cols), jnp.bfloat16),
                pltpu.SemaphoreType.DMA((2,)),
                pltpu.SemaphoreType.DMA((2,)),
            ],
        ),
        compiler_params=pltpu.CompilerParams(vmem_limit_bytes=56 * MIB),
        cost_estimate=pl.CostEstimate(
            flops=4 * all_rows * width * slice_cols * block, transcendentals=0,
            bytes_accessed=60 * MIB,
        ),
    )(where_at, rows, where_at, gathered, tok_t, grad_act, slab)

    partial_grad = pl.pallas_call(
        functools.partial(input_grad_kernel, keep),
        name="token_grad",
        out_shape=jax.ShapeDtypeStruct((all_rows, width), jnp.bfloat16),
        grid_spec=pltpu.PrefetchScalarGridSpec(
            num_scalar_prefetch=2,
            grid=(slice_cols // GROUP,),
            in_specs=[
                pl.BlockSpec((all_rows, cols), lambda i, *_: (0, i)),
                pl.BlockSpec(memory_space=pl.ANY),
            ],
            out_specs=pl.BlockSpec((all_rows, width), lambda i, *_: (0, 0)),
            scratch_shapes=[
                pltpu.VMEM((2, width, cols), jnp.bfloat16),
                pltpu.VMEM((all_rows, width), jnp.float32),
                pltpu.SemaphoreType.DMA((2,)),
            ],
        ),
        compiler_params=pltpu.CompilerParams(vmem_limit_bytes=56 * MIB),
        cost_estimate=pl.CostEstimate(
            flops=2 * all_rows * width * slice_cols * block, transcendentals=0,
            bytes_accessed=30 * MIB,
        ),
    )(where_at, rows, slope, slab)

    grad_tokens = lax.psum_scatter(
        partial_grad.reshape(replicas, tok_rows, width), "replica", scatter_dimension=0, tiled=True
    )
    summed = reduce_blocks(grads.reshape(shards, per_dev, block, block), shards)
    summed = summed.reshape(per_dev, block, block)
    returned = exchange(jnp.take(summed, back_from.reshape(-1), axis=0))
    grad_scale = 1.0 / math.sqrt(replicas * shards * tok_rows)
    mine = jnp.take(returned, slot_from, axis=0).astype(jnp.float32) * grad_scale
    grad_slots = jnp.where(slot_used[:, None, None], mine, 0.0).reshape(1, cap, block, block)
    return (act_out, grad_tokens, grad_slots)


def solution(mesh):
    return jax.shard_map(
        local,
        mesh=mesh,
        in_specs=(
            P("replica", "shard", None),
            P("replica", "shard", None, None),
            P(),
            P(),
            P(),
            P(None, "shard", "replica"),
        ),
        out_specs=(
            P(None, "shard", "replica"),
            P("replica", "shard", None),
            P("replica", "shard", None, None),
        ),
        check_vma=False,
    )
```

time: 1470 us -> 511 us (0.35)
  waiting for transfers between devices: 722 us -> 372 us
  other arithmetic: 308 us -> 18.1 us
  local copies, waits for them, and re-layouts: 276 us -> 22.9 us
  matrix products: 137 us -> 0 us
  Pallas kernels: 0 us -> 71.1 us
    all_gather x2, waiting for transfers between devices: 386 us -> 131 us  [the longest x1 131 us: gather_blocks(): return lax.all_gather(mine, 'shard', axis=0, tiled=False)]
    reduce_scatter x2, waiting for transfers between devices: 334 us -> 135 us  [the longest x1 135 us: reduce_blocks(): return lax.psum_scatter(grads, 'shard', scatter_dimension=0, tiled=False)]
    scatter-add x24 -> x0, other arithmetic: 195 us -> none  [column_step(): grad_rows.at[:, rows_col]]
    dot_general x72 -> x0, matrix products: 137 us -> none  [the longest x24 71.1 us: column_step(): lax.dot_general(col_inputs, slope, (((0,), (0,)), ((), ())), preferred_el...]
    all_to_all x0 -> x2, waiting for transfers between devices: none -> 105 us  [exchange(): return lax.all_to_all(send, 'shard', 0, 0, tiled=True)]
    gather x49 -> x7, local copies, waits for them, and re-layouts: 99.2 us -> 15.5 us  [the longest x1 4.09 us: local(): jnp.take(returned, slot_from, axis=0).astype(jnp.float32) * grad_scale]
    pallas_call x0 -> x2, Pallas kernels: none -> 71.1 us  [the longest x1 45.6 us: local(): pl.pallas_call(functools.partial(forward_kernel, keep), name='forward_and...]
    select_n x74 -> x8, other arithmetic: 67.7 us -> 8.7 us  [the longest x2 3.36 us: local(): returned = exchange(jnp.take(summed, back_from.reshape(-1), axis=0))]
  transfers between devices with their start and end apart: 4 -> 6, of which waited for: 4 -> 4; matrix products, arithmetic and copies ran while one was open for 2% -> 8% of each run, Pallas kernels for 0% -> 5%
where the time goes in v1:
time: 511 us; the launch traced here: 510 us
  waiting for transfers between devices  372 us (73%)
  Pallas kernels  71.1 us (14%)
  local copies, waits for them, and re-layouts  22.9 us (4%)
  other arithmetic  18.1 us (4%)
  between operations  14 us (3%)
  starting transfers between devices  12 us (2%)
    reduce_scatter x1, waiting for transfers between devices, reduce_blocks(): return lax.psum_scatter(grads, 'shard', scatter_dimension=0, tiled=False)  135 us
    all_gather x1, waiting for transfers between devices, gather_blocks(): return lax.all_gather(mine, 'shard', axis=0, tiled=False)  131 us
    all_to_all x2, waiting for transfers between devices, exchange(): return lax.all_to_all(send, 'shard', 0, 0, tiled=True)  105 us
    pallas_call x1, Pallas kernels, local(): pl.pallas_call(functools.partial(forward_kernel, keep), name='forward_and...  45.6 us
    pallas_call x1, Pallas kernels, local(): pl.pallas_call(functools.partial(input_grad_kernel, keep), name='token_gr...  25.5 us
    all_to_all x2, starting transfers between devices, exchange(): return lax.all_to_all(send, 'shard', 0, 0, tiled=True)  11.9 us
  transfers between devices with their start and end apart: 6, of which 4 were waited for; matrix products, arithmetic and copies ran while one was open for 8% of the time, Pallas kernels for 5%

profile of v1, /device:TPU:0, one launch (start us, length us, event | category | flops | bytes accessed | tf_op | source)
XLA Modules:
  0.0 509.9 jit_solution(11420126955171677589)
XLA Ops:
  7.2 0.7 all-gather.3.cloned.1.call-update
  8.0 0.8 dynamic-slice_add_fusion
  8.9 0.2 convert_reduce_fusion
  9.2 0.2 convert_reduce_fusion.2
  9.3 0.6 dynamic_slice.15
  10.0 1.2 fusion.4
  11.7 1.3 gather_fusion.2
  13.1 2.4 gather_fusion.5
  15.5 3.3 broadcast_select_fusion
  18.8 7.4 %all-to-all-start = ((bf16[72,128,128]{2,1,0:T(8,128)(2,1)}), bf16[72,128,128]{2,1,0:T(8,128)(2,1)}, u32[]{:S(2)}, u32[]{:S(2)}) async-start(bf16[72,128,128]{2,1,0:T(8,128)(2,1)} %broadcast_select_fusion), calls=%async_computation | async-start | bytes 4718592 | tf_op jit(solution)/shard_map/all_to_all | solution.py:164
  26.3 0.8 gather_fusion
  27.1 0.8 gather_fusion.1
  28.0 0.5 compare_and_fusion.3
  28.5 51.6 %all-to-all-done = bf16[72,128,128]{2,1,0:T(8,128)(2,1)} async-done(((bf16[72,128,128]{2,1,0:T(8,128)(2,1)}), bf16[72,128,128]{2,1,0:T(8,128)(2,1)}, u32[]{:S(2)}, u32[]{:S(2)}) %all-to-all-start) | async-done | bytes 2359328 | tf_op jit(solution)/shard_map/all_to_all | solution.py:164
  80.1 2.4 gather_fusion.3
  82.5 1.8 bitcast_select_fusion
  84.6 0.7 reshape.447.rows_ref
  85.3 0.6 fusion.1.idx_ref.pos_ref
  85.9 4.6 copy.23
  90.5 131.2 %all-gather.5.cloned.1.call-done = bf16[8,36,128,128]{3,2,1,0:T(8,128)(2,1)} async-done(((bf16[1,36,128,128]{3,2,1,0:T(8,128)(2,1)}), bf16[8,36,128,128]{3,2,1,0:T(8,128)(2,1)}) %all-gather.5.cloned.1.call-update) | async-done | bytes 9437200 | tf_op jit(solution)/shard_map/all_gather | solution.py:156
  221.7 45.6 %forward_and_weight_grad.1 = (bf16[4,128,3072]{2,1,0:T(8,128)(2,1)}, bf16[512,3072]{1,0:T(8,128)(2,1)}, bf16[288,128,128]{2,1,0:T(8,128)(2,1)}) custom-call(s32[288]{0:T(512)} %fusion.1.idx_ref.pos_ref, s32[288]{0:T(512)} %reshape.447.rows_ref, s32[288]{0:T(512)} %fusion.1.idx_ref.pos_ref, bf16[512,3072]{1,0:T(8,128)(2,1)} %bitcast.40, ...), custom_call_target="tpu_custom_call" | custom-call | flops 19327352832 | bytes 62914560 | tf_op jit(solution)/shard_map/forward_and_weight_grad/pallas_call | solution.py:218
  267.4 25.5 %token_grad.1 = bf16[512,3072]{1,0:T(8,128)(2,1)} custom-call(s32[288]{0:T(512)} %fusion.1.idx_ref.pos_ref, s32[288]{0:T(512)} %reshape.447.rows_ref, bf16[512,3072]{1,0:T(8,128)(2,1)} %get-tuple-element.8.slope_ref, bf16[288,128,128]{2,1,0:T(8,128)(2,1)} %bitcast.44), custom_call_target="tpu_custom_call" | custom-call | flops 9663676416 | bytes 31457280 | tf_op jit(solution)/shard_map/token_grad/pallas_call | solution.py:254
  293.0 0.6 copy-done.3
  293.9 135.2 %reduce-scatter.5.cloned.1.call-done = bf16[1,36,128,128]{3,2,1,0:T(8,128)(2,1)} async-done(((bf16[8,36,128,128]{3,2,1,0:T(8,128)(2,1)}), bf16[1,36,128,128]{3,2,1,0:T(8,128)(2,1)}) %reduce-scatter.5.cloned.1.call-update) | async-done | bytes 1179664 | tf_op jit(solution)/shard_map/reduce_scatter | solution.py:160
  429.1 3.7 gather_fusion.4
  432.8 3.3 broadcast_select_fusion.1
  436.1 4.5 all-to-all-start.1
  440.8 0.7 compare_and_fusion
  441.5 0.2 compare_reduce_fusion
  441.7 53.0 %all-to-all-done.1 = bf16[72,128,128]{2,1,0:T(8,128)(2,1)} async-done(((bf16[72,128,128]{2,1,0:T(8,128)(2,1)}), bf16[72,128,128]{2,1,0:T(8,128)(2,1)}, u32[]{:S(2)}, u32[]{:S(2)}) %all-to-all-start.1) | async-done | bytes 2359328 | tf_op jit(solution)/shard_map/all_to_all | solution.py:164
  494.7 4.1 gather_fusion.6
  498.8 4.6 select_bitcast_fusion
  (49 shorter events, 1.7 us)
Async XLA Ops:
  7.2 5.9 %copy-start = (bf16[1,72,128,128]{3,2,1,0:T(8,128)(2,1)S(1)}, bf16[1,72,128,128]{3,2,1,0:T(8,128)(2,1)}, u32[]{:S(2)}) copy-start(bf16[1,72,128,128]{3,2,1,0:T(8,128)(2,1)} %param.9) | copy-start | bytes 7077892
  7.2 78.7 %all-gather.3.cloned.1.call-start = ((), (), s32[]{:S(2)}) async-start(), calls=%async_computation.4 | async-start | bytes 3932160 | tf_op jit(solution)/shard_map/all_gather | solution.py:210
  7.9 7.6 %copy-start.2 = (s32[9]{0:T(128)}, s32[9]{0:T(128)S(1)}, u32[]{:S(2)}) copy-start(s32[9]{0:T(128)S(1)} %iota_multiply_fusion) | copy-start | bytes 112
  18.8 61.2 %all-to-all-start = ((bf16[72,128,128]{2,1,0:T(8,128)(2,1)}), bf16[72,128,128]{2,1,0:T(8,128)(2,1)}, u32[]{:S(2)}, u32[]{:S(2)}) async-start(bf16[72,128,128]{2,1,0:T(8,128)(2,1)} %broadcast_select_fusion), calls=%async_computation | async-start | bytes 4718592 | tf_op jit(solution)/shard_map/all_to_all | solution.py:164
  26.2 195.5 %all-gather.5.cloned.1.call-start = ((), (), s32[]{:S(2)}) async-start(), calls=%async_computation.5 | async-start | bytes 10616832 | tf_op jit(solution)/shard_map/all_gather | solution.py:156
  82.5 1.9 copy-start.1
  84.4 344.6 %reduce-scatter.5.cloned.1.call-start = ((), (), s32[]{:S(2)}) async-start(), calls=%async_computation.7 | async-start | bytes 10616832 | tf_op jit(solution)/shard_map/reduce_scatter | solution.py:160
  267.3 236.0 %reduce-scatter.3.cloned.1.call-start = ((), (), s32[]{:S(2)}) async-start(), calls=%async_computation.6 | async-start | bytes 3932160 | tf_op jit(solution)/shard_map/reduce_scatter | solution.py:279
  292.9 0.7 copy-start.3
  292.9 0.7 copy-start.4
  436.1 58.6 %all-to-all-start.1 = ((bf16[72,128,128]{2,1,0:T(8,128)(2,1)}), bf16[72,128,128]{2,1,0:T(8,128)(2,1)}, u32[]{:S(2)}, u32[]{:S(2)}) async-start(bf16[72,128,128]{2,1,0:T(8,128)(2,1)} %broadcast_select_fusion.1), calls=%async_computation.3 | async-start | bytes 4718592 | tf_op jit(solution)/shard_map/all_to_all | solution.py:164
Sparse Core Ops, SparseCore 0:
  9.6 31.2 all-gather.2
  84.5 137.1 all-gather.4
  267.5 161.5 reduce-scatter.4
  432.0 37.0 reduce-scatter.2

commit v2 on v1

--- a/solution.py
+++ b/solution.py
@@ -10,6 +10,7 @@
 
 GROUP = 4
 PIECES = 6
+CROSS_FIRST = 3
 MIB = 1 << 20
 
 
@@ -152,12 +153,309 @@
         out_ref[...] = total[...].astype(out_ref.dtype)
 
 
-def gather_blocks(mine, shard_count):
-    return lax.all_gather(mine, "shard", axis=0, tiled=False)
-
-
-def reduce_blocks(grads, shard_count):
-    return lax.psum_scatter(grads, "shard", scatter_dimension=0, tiled=False)
+def neighbours(shards):
+    me = lax.axis_index("shard")
+    return me, me // 2, lax.rem(me, 2), shards // 2
+
+
+def greet(me, line, length):
+    barrier = pltpu.get_barrier_semaphore()
+    other = me + 1 - 2 * lax.rem(me, 2)
+
+    def tell(to):
+        pl.semaphore_signal(barrier, inc=1, device_id={"shard": to},
+                            device_id_type=pl.DeviceIdType.MESH)
+
+    tell(other)
+
+    @pl.when(line < length - 1)
+    def _():
+        tell(me + 2)
+
+    @pl.when(line > 0)
+    def _():
+        tell(me - 2)
+
+    pl.semaphore_wait(
+        barrier, 1 + (line < length - 1).astype(jnp.int32) + (line > 0).astype(jnp.int32))
+    return other
+
+
+UP, DOWN, ACROSS = 0, 1, 2
+
+
+def gather_kernel(shards, held_ref, slab_ref, send_sem, recv_sem, own_sem):
+    me, line, _, length = neighbours(shards)
+    size = held_ref.shape[0] // PIECES
+    own = pltpu.make_async_copy(held_ref, slab_ref.at[me], own_sem)
+    own.start()
+    other = greet(me, line, length)
+    targets = (me + 2, me - 2, other)
+
+    def copy(way, source, piece):
+        at = pl.ds(piece * size, size)
+        return pltpu.make_async_remote_copy(
+            src_ref=slab_ref.at[source, at], dst_ref=slab_ref.at[source, at],
+            send_sem=send_sem.at[way, source, piece], recv_sem=recv_sem.at[source, piece],
+            device_id={"shard": targets[way]}, device_id_type=pl.DeviceIdType.MESH,
+        )
+
+    def for_each(first, last, body):
+        def step(piece, carry):
+            body(piece)
+            return carry
+
+        lax.fori_loop(first, last, step, 0)
+
+    def relay(act):
+        start, arrive = act
+
+        def own_piece(piece):
+            @pl.when(line < length - 1)
+            def _():
+                start(UP, me, piece)
+
+            @pl.when(line > 0)
+            def _():
+                start(DOWN, me, piece)
+
+            start(ACROSS, me, piece)
+
+        for_each(0, PIECES, own_piece)
+        for far in range(1, length):
+
+            def column(piece, far=far):
+                @pl.when(line >= far)
+                def _():
+                    arrive(me - 2 * far, piece)
+
+                    @pl.when(line < length - 1)
+                    def _():
+                        start(UP, me - 2 * far, piece)
+
+                    @pl.when(piece >= CROSS_FIRST)
+                    def _():
+                        start(ACROSS, me - 2 * far, piece)
+
+                @pl.when(line + far < length)
+                def _():
+                    arrive(me + 2 * far, piece)
+
+                    @pl.when(line > 0)
+                    def _():
+                        start(DOWN, me + 2 * far, piece)
+
+                    @pl.when(piece >= CROSS_FIRST)
+                    def _():
+                        start(ACROSS, me + 2 * far, piece)
+
+                if far == 1:
+                    arrive(other, piece)
+
+                    @pl.when(piece < CROSS_FIRST)
+                    def _():
+                        @pl.when(line < length - 1)
+                        def _():
+                            start(UP, other, piece)
+
+                        @pl.when(line > 0)
+                        def _():
+                            start(DOWN, other, piece)
+
+            for_each(0, PIECES, column)
+
+            def crossed(piece, far=far):
+                @pl.when(line >= far)
+                def _():
+                    arrive(other - 2 * far, piece)
+
+                    @pl.when(line < length - 1)
+                    def _():
+                        start(UP, other - 2 * far, piece)
+
+                @pl.when(line + far < length)
+                def _():
+                    arrive(other + 2 * far, piece)
+
+                    @pl.when(line > 0)
+                    def _():
+                        start(DOWN, other + 2 * far, piece)
+
+            for_each(0, CROSS_FIRST, crossed)
+        for far in range(1, length):
+
+            def last(piece, far=far):
+                @pl.when(line >= far)
+                def _():
+                    arrive(other - 2 * far, piece)
+
+                @pl.when(line + far < length)
+                def _():
+                    arrive(other + 2 * far, piece)
+
+            for_each(CROSS_FIRST, PIECES, last)
+
+    own.wait()
+    relay((lambda way, source, piece: copy(way, source, piece).start(),
+           lambda source, piece: copy(ACROSS, source, piece).wait_recv()))
+    relay((lambda way, source, piece: copy(way, source, piece).wait_send(),
+           lambda source, piece: None))
+
+
+def gather_blocks(held, shards):
+    return pl.pallas_call(
+        functools.partial(gather_kernel, shards),
+        name="gather_blocks",
+        out_shape=jax.ShapeDtypeStruct((shards,) + held.shape, held.dtype),
+        in_specs=[pl.BlockSpec(memory_space=pl.ANY)],
+        out_specs=pl.BlockSpec(memory_space=pl.ANY),
+        scratch_shapes=[
+            pltpu.SemaphoreType.DMA((3, shards, PIECES)),
+            pltpu.SemaphoreType.DMA((shards, PIECES)),
+            pltpu.SemaphoreType.DMA,
+        ],
+        compiler_params=pltpu.CompilerParams(collective_id=0, has_side_effects=True),
+    )(held)
+
+
+def reduce_kernel(shards, grads_ref, out_ref, acc, below, above, across,
+                  send_sem, below_sem, above_sem, across_sem, load_sem):
+    me, line, side, length = neighbours(shards)
+    size = out_ref.shape[0] // PIECES
+    load = pltpu.make_async_copy(grads_ref, acc, load_sem)
+    load.start()
+    other = greet(me, line, length)
+    load.wait()
+
+    def part(piece):
+        return pl.ds(piece * size, size)
+
+    def copy(way, dest, piece):
+        landing, sem, to = (
+            (below, below_sem, me + 2),
+            (above, above_sem, me - 2),
+            (across, across_sem, other),
+        )[way]
+        return pltpu.make_async_remote_copy(
+            src_ref=acc.at[dest, part(piece)], dst_ref=landing.at[dest, part(piece)],
+            send_sem=send_sem.at[dest, piece], recv_sem=sem.at[dest, piece],
+            device_id={"shard": to}, device_id_type=pl.DeviceIdType.MESH,
+        )
+
+    def for_each(first, last, body):
+        def step(piece, carry):
+            body(piece)
+            return carry
+
+        lax.fori_loop(first, last, step, 0)
+
+    def add(way, dest, piece):
+        copy(way, dest, piece).wait_recv()
+        landing = (below, above, across)[way]
+        total = (acc[dest, part(piece)].astype(jnp.float32)
+                 + landing[dest, part(piece)].astype(jnp.float32))
+        acc[dest, part(piece)] = total.astype(acc.dtype)
+
+    def schedule(start, add):
+        for far in range(length - 1, -1, -1):
+
+            def cross(piece, far=far):
+                @pl.when(line + far < length)
+                def _():
+                    start(ACROSS, other + 2 * far, piece)
+
+                if far > 0:
+                    @pl.when(line >= far)
+                    def _():
+                        start(ACROSS, other - 2 * far, piece)
+
+            for_each(CROSS_FIRST, PIECES, cross)
+        for far in range(length - 1, 0, -1):
+
+            def along(piece, column, far=far):
+                @pl.when(line + far < length)
+                def _():
+                    dest = column + 2 * far
+
+                    @pl.when(piece >= CROSS_FIRST)
+                    def _():
+                        add(ACROSS, dest, piece)
+
+                    @pl.when(line > 0)
+                    def _():
+                        add(UP, dest, piece)
+
+                    start(UP, dest, piece)
+
+                @pl.when(line >= far)
+                def _():
+                    dest = column - 2 * far
+
+                    @pl.when(piece >= CROSS_FIRST)
+                    def _():
+                        add(ACROSS, dest, piece)
+
+                    @pl.when(line < length - 1)
+                    def _():
+                        add(DOWN, dest, piece)
+
+                    start(DOWN, dest, piece)
+
+            def both(piece):
+                along(piece, other)
+                along(piece, me)
+
+            for_each(0, CROSS_FIRST, both)
+            for_each(CROSS_FIRST, PIECES, functools.partial(along, column=me))
+
+        def turn(piece):
+            @pl.when(line > 0)
+            def _():
+                add(UP, other, piece)
+
+            @pl.when(line < length - 1)
+            def _():
+                add(DOWN, other, piece)
+
+            start(ACROSS, other, piece)
+
+        for_each(0, CROSS_FIRST, turn)
+
+    schedule(lambda way, dest, piece: copy(way, dest, piece).start(), add)
+
+    def finish(piece):
+        @pl.when(line > 0)
+        def _():
+            add(UP, me, piece)
+
+        @pl.when(line < length - 1)
+        def _():
+            add(DOWN, me, piece)
+
+        add(ACROSS, me, piece)
+        out_ref[part(piece)] = acc[me, part(piece)]
+
+    for_each(CROSS_FIRST, PIECES, finish)
+    for_each(0, CROSS_FIRST, finish)
+    schedule(lambda way, dest, piece: copy(way, dest, piece).wait_send(),
+             lambda way, dest, piece: None)
+
+
+def reduce_blocks(grads, shards):
+    shape = grads.shape
+    sems = pltpu.SemaphoreType.DMA((shards, PIECES))
+    buffer = pltpu.VMEM(shape, grads.dtype)
+    return pl.pallas_call(
+        functools.partial(reduce_kernel, shards),
+        name="reduce_blocks",
+        out_shape=jax.ShapeDtypeStruct(shape[1:], grads.dtype),
+        in_specs=[pl.BlockSpec(memory_space=pl.ANY)],
+        out_specs=pl.BlockSpec(memory_space=pltpu.VMEM),
+        scratch_shapes=[buffer, buffer, buffer, buffer, sems, sems, sems, sems,
+                        pltpu.SemaphoreType.DMA],
+        compiler_params=pltpu.CompilerParams(
+            collective_id=1, has_side_effects=True, vmem_limit_bytes=56 * MIB),
+    )(grads)
 
 
 def exchange(send):

time: 511 us -> 515 us (level)
  Pallas kernels: 71.1 us -> 345 us
  waiting for transfers between devices: 372 us -> 103 us
    pallas_call x0 -> x2, Pallas kernels: none -> 274 us  [the longest x1 154 us: gather_blocks(): pl.pallas_call(functools.partial(gather_kernel, shards), name='gather_blo...]
    reduce_scatter x1 -> x0, waiting for transfers between devices: 135 us -> none  [reduce_blocks(): return lax.psum_scatter(grads, 'shard', scatter_dimension=0, tiled=False)]
    all_gather x1 -> x0, waiting for transfers between devices: 131 us -> none  [gather_blocks(): return lax.all_gather(mine, 'shard', axis=0, tiled=False)]
  transfers between devices with their start and end apart: 6 -> 4, of which waited for: 4 -> 2; matrix products, arithmetic and copies ran while one was open for 8% -> 7% of each run, Pallas kernels for 5% -> 53%
where the time goes in v2:
time: 515 us; the launch traced here: 514 us
  Pallas kernels  345 us (67%)
  waiting for transfers between devices  103 us (20%)
  local copies, waits for them, and re-layouts  22.2 us (4%)
  other arithmetic  16.8 us (3%)
  between operations  14.2 us (3%)
  starting transfers between devices  12.6 us (2%)
    pallas_call x1, Pallas kernels, gather_blocks(): pl.pallas_call(functools.partial(gather_kernel, shards), name='gather_blo...  154 us
    pallas_call x1, Pallas kernels, reduce_blocks(): pl.pallas_call(functools.partial(reduce_kernel, shards), name='reduce_blo...  120 us
    all_to_all x2, waiting for transfers between devices, exchange(): return lax.all_to_all(send, 'shard', 0, 0, tiled=True)  103 us
    pallas_call x1, Pallas kernels, local(): pl.pallas_call(functools.partial(forward_kernel, keep), name='forward_and...  45.5 us
    pallas_call x1, Pallas kernels, local(): pl.pallas_call(functools.partial(input_grad_kernel, keep), name='token_gr...  25.6 us
    all_to_all x2, starting transfers between devices, exchange(): return lax.all_to_all(send, 'shard', 0, 0, tiled=True)  12.5 us
  transfers between devices with their start and end apart: 4, of which 2 were waited for; matrix products, arithmetic and copies ran while one was open for 7% of the time, Pallas kernels for 53%

profile of v2, /device:TPU:0, one launch (start us, length us, event | category | flops | bytes accessed | tf_op | source)
XLA Modules:
  0.0 513.9 jit_solution(8364016451039284768)
XLA Ops:
  7.2 0.7 all-gather.2.cloned.1.call-update
  7.9 0.8 dynamic-slice_add_fusion
  8.9 0.2 convert_reduce_fusion
  9.1 0.2 convert_reduce_fusion.2
  9.3 0.6 dynamic_slice.15
  9.9 0.6 fusion.6
  11.2 1.3 gather_fusion.2
  12.5 0.6 compare_and_fusion.1
  13.1 2.4 gather_fusion.5
  15.5 3.3 broadcast_select_fusion
  18.8 7.5 %all-to-all-start = ((bf16[72,128,128]{2,1,0:T(8,128)(2,1)}), bf16[72,128,128]{2,1,0:T(8,128)(2,1)}, u32[]{:S(2)}, u32[]{:S(2)}) async-start(bf16[72,128,128]{2,1,0:T(8,128)(2,1)} %broadcast_select_fusion), calls=%async_computation | async-start | bytes 4718592 | tf_op jit(solution)/shard_map/all_to_all | solution.py:462
  26.4 0.8 gather_fusion
  27.3 0.8 gather_fusion.1
  28.2 0.7 reshape.440.rows_ref
  29.0 0.6 fusion.1.idx_ref.pos_ref
  29.6 50.7 %all-to-all-done = bf16[72,128,128]{2,1,0:T(8,128)(2,1)} async-done(((bf16[72,128,128]{2,1,0:T(8,128)(2,1)}), bf16[72,128,128]{2,1,0:T(8,128)(2,1)}, u32[]{:S(2)}, u32[]{:S(2)}) %all-to-all-start) | async-done | bytes 2359328 | tf_op jit(solution)/shard_map/all_to_all | solution.py:462
  80.2 2.4 gather_fusion.3
  82.7 1.2 broadcast_select_fusion.2.held_ref
  83.9 153.5 %gather_blocks.1 = bf16[8,36,128,128]{3,2,1,0:T(8,128)(2,1)} custom-call(bf16[36,128,128]{2,1,0:T(8,128)(2,1)} %broadcast_select_fusion.2.held_ref), custom_call_target="tpu_custom_call" | custom-call | tf_op jit(solution)/shard_map/gather_blocks/pallas_call | solution.py:306
  237.4 4.6 copy.23
  242.1 45.5 %forward_and_weight_grad.1 = (bf16[4,128,3072]{2,1,0:T(8,128)(2,1)}, bf16[512,3072]{1,0:T(8,128)(2,1)}, bf16[288,128,128]{2,1,0:T(8,128)(2,1)}) custom-call(s32[288]{0:T(512)} %fusion.1.idx_ref.pos_ref, s32[288]{0:T(512)} %reshape.440.rows_ref, s32[288]{0:T(512)} %fusion.1.idx_ref.pos_ref, bf16[512,3072]{1,0:T(8,128)(2,1)} %bitcast.38, ...), custom_call_target="tpu_custom_call" | custom-call | flops 19327352832 | bytes 62914560 | tf_op jit(solution)/shard_map/forward_and_weight_grad/pallas_call | solution.py:516
  287.6 25.6 %token_grad.1 = bf16[512,3072]{1,0:T(8,128)(2,1)} custom-call(s32[288]{0:T(512)} %fusion.1.idx_ref.pos_ref, s32[288]{0:T(512)} %reshape.440.rows_ref, bf16[512,3072]{1,0:T(8,128)(2,1)} %get-tuple-element.8.slope_ref, bf16[288,128,128]{2,1,0:T(8,128)(2,1)} %bitcast.36), custom_call_target="tpu_custom_call" | custom-call | flops 9663676416 | bytes 31457280 | tf_op jit(solution)/shard_map/token_grad/pallas_call | solution.py:552
  313.3 120.1 %reduce_blocks.1 = bf16[36,128,128]{2,1,0:T(8,128)(2,1)} custom-call(bf16[8,36,128,128]{3,2,1,0:T(8,128)(2,1)} %bitcast.34), custom_call_target="tpu_custom_call" | custom-call | tf_op jit(solution)/shard_map/reduce_blocks/pallas_call | solution.py:448
  433.4 3.7 gather_fusion.4
  437.1 3.3 broadcast_select_fusion.1
  440.4 5.0 all-to-all-start.1
  445.5 0.2 convert_reduce_fusion.1
  445.6 0.6 compare_and_fusion
  446.2 0.2 compare_reduce_fusion
  446.4 52.0 %all-to-all-done.1 = bf16[72,128,128]{2,1,0:T(8,128)(2,1)} async-done(((bf16[72,128,128]{2,1,0:T(8,128)(2,1)}), bf16[72,128,128]{2,1,0:T(8,128)(2,1)}, u32[]{:S(2)}, u32[]{:S(2)}) %all-to-all-start.1) | async-done | bytes 2359328 | tf_op jit(solution)/shard_map/all_to_all | solution.py:462
  498.5 4.1 gather_fusion.6
  502.5 4.6 select_bitcast_fusion
  (41 shorter events, 1.4 us)
Async XLA Ops:
  7.2 5.9 %copy-start = (bf16[1,72,128,128]{3,2,1,0:T(8,128)(2,1)S(1)}, bf16[1,72,128,128]{3,2,1,0:T(8,128)(2,1)}, u32[]{:S(2)}) copy-start(bf16[1,72,128,128]{3,2,1,0:T(8,128)(2,1)} %param.9) | copy-start | bytes 7077892
  7.2 230.2 %all-gather.2.cloned.1.call-start = ((), (), s32[]{:S(2)}) async-start(), calls=%async_computation.3 | async-start | bytes 3932160 | tf_op jit(solution)/shard_map/all_gather | solution.py:508
  18.8 9.2 %copy-start.1 = (s32[96,12]{0,1:T(8,128)S(1)}, s32[96,12]{0,1:T(8,128)}, u32[]{:S(2)}) copy-start(s32[96,12]{0,1:T(8,128)} %param.10) | copy-start | bytes 13828
  18.8 61.4 %all-to-all-start = ((bf16[72,128,128]{2,1,0:T(8,128)(2,1)}), bf16[72,128,128]{2,1,0:T(8,128)(2,1)}, u32[]{:S(2)}, u32[]{:S(2)}) async-start(bf16[72,128,128]{2,1,0:T(8,128)(2,1)} %broadcast_select_fusion), calls=%async_computation | async-start | bytes 4718592 | tf_op jit(solution)/shard_map/all_to_all | solution.py:462
  26.4 480.8 %reduce-scatter.2.cloned.1.call-start = ((), (), s32[]{:S(2)}) async-start(), calls=%async_computation.4 | async-start | bytes 3932160 | tf_op jit(solution)/shard_map/reduce_scatter | solution.py:577
  433.4 3.7 copy-start.2
  440.4 58.0 %all-to-all-start.1 = ((bf16[72,128,128]{2,1,0:T(8,128)(2,1)}), bf16[72,128,128]{2,1,0:T(8,128)(2,1)}, u32[]{:S(2)}, u32[]{:S(2)}) async-start(bf16[72,128,128]{2,1,0:T(8,128)(2,1)} %broadcast_select_fusion.1), calls=%async_computation.2 | async-start | bytes 4718592 | tf_op jit(solution)/shard_map/all_to_all | solution.py:462
Sparse Core Ops, SparseCore 0:
  9.6 31.2 all-gather.1
  313.3 36.1 reduce-scatter.1

commit v3 on v1

--- a/solution.py
+++ b/solution.py
@@ -10,6 +10,7 @@
 
 GROUP = 4
 PIECES = 6
+SPLIT = 3
 MIB = 1 << 20
 
 
@@ -152,12 +153,189 @@
         out_ref[...] = total[...].astype(out_ref.dtype)
 
 
-def gather_blocks(mine, shard_count):
-    return lax.all_gather(mine, "shard", axis=0, tiled=False)
-
-
-def reduce_blocks(grads, shard_count):
-    return lax.psum_scatter(grads, "shard", scatter_dimension=0, tiled=False)
+def ring_index(position, shards):
+    position = lax.rem(position + shards, shards)
+    half = shards // 2
+    side = position // half
+    return 2 * (position + side * (shards - 1 - 2 * position)) + side
+
+
+def ring_place(shards):
+    me = lax.axis_index("shard")
+    line, side = me // 2, lax.rem(me, 2)
+    here = line + side * (shards - 1 - 2 * line)
+    ways = (ring_index(here + 1, shards), ring_index(here - 1, shards))
+    barrier = pltpu.get_barrier_semaphore()
+    for to in ways:
+        pl.semaphore_signal(barrier, inc=1, device_id={"shard": to},
+                            device_id_type=pl.DeviceIdType.MESH)
+    pl.semaphore_wait(barrier, 2)
+    return me, here, ways
+
+
+def for_each(first, last, body):
+    def step(piece, carry):
+        body(piece)
+        return carry
+
+    lax.fori_loop(first, last, step, 0)
+
+
+NEXT, LAST = 0, 1
+SIGN = (1, -1)
+
+
+def hop_pieces(way, hop, shards):
+    if hop < shards // 2:
+        return (0, PIECES)
+    if hop > shards // 2:
+        return (0, 0)
+    return ((0, SPLIT), (SPLIT, PIECES))[way]
+
+
+def gather_kernel(shards, held_ref, slab_ref, send_sem, recv_sem, own_sem):
+    size = held_ref.shape[0] // PIECES
+    me, here, ways = ring_place(shards)
+    own = pltpu.make_async_copy(held_ref, slab_ref.at[me], own_sem)
+    own.start()
+    own.wait()
+
+    def copy(way, source, piece):
+        at = pl.ds(piece * size, size)
+        return pltpu.make_async_remote_copy(
+            src_ref=slab_ref.at[source, at], dst_ref=slab_ref.at[source, at],
+            send_sem=send_sem.at[way, source, piece], recv_sem=recv_sem.at[source, piece],
+            device_id={"shard": ways[way]}, device_id_type=pl.DeviceIdType.MESH,
+        )
+
+    def source(way, hop):
+        return ring_index(here - SIGN[way] * hop, shards)
+
+    def own_piece(piece):
+        for way in (NEXT, LAST):
+            copy(way, me, piece).start()
+
+    for_each(0, PIECES, own_piece)
+    for hop in range(1, shards // 2 + 1):
+
+        def relay(piece, hop=hop):
+            for way in (NEXT, LAST):
+                first, last = hop_pieces(way, hop, shards)
+
+                @pl.when((piece >= first) & (piece < last))
+                def _(way=way):
+                    copy(way, source(way, hop), piece).wait_recv()
+
+                first, last = hop_pieces(way, hop + 1, shards)
+                if last > first:
+
+                    @pl.when((piece >= first) & (piece < last))
+                    def _(way=way):
+                        copy(way, source(way, hop), piece).start()
+
+        for_each(0, PIECES, relay)
+    for hop in range(1, shards // 2 + 1):
+        for way in (NEXT, LAST):
+            for_each(*hop_pieces(way, hop, shards),
+                     lambda piece, way=way, hop=hop:
+                     copy(way, source(way, hop - 1), piece).wait_send())
+
+
+def gather_blocks(held, shards):
+    return pl.pallas_call(
+        functools.partial(gather_kernel, shards),
+        name="gather_blocks",
+        out_shape=jax.ShapeDtypeStruct((shards,) + held.shape, held.dtype),
+        in_specs=[pl.BlockSpec(memory_space=pl.ANY)],
+        out_specs=pl.BlockSpec(memory_space=pl.ANY),
+        scratch_shapes=[
+            pltpu.SemaphoreType.DMA((2, shards, PIECES)),
+            pltpu.SemaphoreType.DMA((shards, PIECES)),
+            pltpu.SemaphoreType.DMA,
+        ],
+        compiler_params=pltpu.CompilerParams(collective_id=0, has_side_effects=True),
+    )(held)
+
+
+def reduce_kernel(shards, grads_ref, out_ref, acc, landing, send_sem, recv_sem, load_sem):
+    size = out_ref.shape[0] // PIECES
+    load = pltpu.make_async_copy(grads_ref, acc, load_sem)
+    load.start()
+    me, here, ways = ring_place(shards)
+    load.wait()
+
+    def part(piece):
+        return pl.ds(piece * size, size)
+
+    def copy(way, dest, piece):
+        return pltpu.make_async_remote_copy(
+            src_ref=acc.at[dest, part(piece)], dst_ref=landing.at[way, dest, part(piece)],
+            send_sem=send_sem.at[dest, piece], recv_sem=recv_sem.at[way, dest, piece],
+            device_id={"shard": ways[way]}, device_id_type=pl.DeviceIdType.MESH,
+        )
+
+    def dest_at(way, hop):
+        return ring_index(here + SIGN[way] * hop, shards)
+
+    def add(way, dest, piece):
+        copy(way, dest, piece).wait_recv()
+        total = (acc[dest, part(piece)].astype(jnp.float32)
+                 + landing[way, dest, part(piece)].astype(jnp.float32))
+        acc[dest, part(piece)] = total.astype(acc.dtype)
+
+    for hop in range(shards // 2, 0, -1):
+
+        def relay(piece, hop=hop):
+            for way in (NEXT, LAST):
+                dest = dest_at(way, hop)
+                first, last = hop_pieces(way, hop + 1, shards)
+                if last > first:
+
+                    @pl.when((piece >= first) & (piece < last))
+                    def _(way=way, dest=dest):
+                        add(way, dest, piece)
+
+                first, last = hop_pieces(way, hop, shards)
+
+                @pl.when((piece >= first) & (piece < last))
+                def _(way=way, dest=dest):
+                    copy(way, dest, piece).start()
+
+        for_each(0, PIECES, relay)
+
+    def finish(piece):
+        total = acc[me, part(piece)].astype(jnp.float32)
+        for way in (NEXT, LAST):
+            copy(way, me, piece).wait_recv()
+            total = total + landing[way, me, part(piece)].astype(jnp.float32)
+        out_ref[part(piece)] = total.astype(out_ref.dtype)
+
+    for_each(0, PIECES, finish)
+    for hop in range(shards // 2, 0, -1):
+        for way in (NEXT, LAST):
+            for_each(*hop_pieces(way, hop, shards),
+                     lambda piece, way=way, hop=hop:
+                     copy(way, dest_at(way, hop), piece).wait_send())
+
+
+def reduce_blocks(grads, shards):
+    shape = grads.shape
+    return pl.pallas_call(
+        functools.partial(reduce_kernel, shards),
+        name="reduce_blocks",
+        out_shape=jax.ShapeDtypeStruct(shape[1:], grads.dtype),
+        in_specs=[pl.BlockSpec(memory_space=pl.ANY)],
+        out_specs=pl.BlockSpec(memory_space=pltpu.VMEM),
+        scratch_shapes=[
+            pltpu.VMEM(shape, grads.dtype),
+            pltpu.VMEM((2,) + shape, grads.dtype),
+            pltpu.SemaphoreType.DMA((shards, PIECES)),
+            pltpu.SemaphoreType.DMA((2, shards, PIECES)),
+            pltpu.SemaphoreType.DMA,
+        ],
+        compiler_params=pltpu.CompilerParams(
+            collective_id=1, has_side_effects=True, vmem_limit_bytes=56 * MIB),
+    )(grads)
 
 
 def exchange(send):

time: 511 us -> 466 us (0.912)
  waiting for transfers between devices: 372 us -> 103 us
  Pallas kernels: 71.1 us -> 297 us
    pallas_call x0 -> x2, Pallas kernels: none -> 226 us  [the longest x1 129 us: gather_blocks(): pl.pallas_call(functools.partial(gather_kernel, shards), name='gather_blo...]
    reduce_scatter x1 -> x0, waiting for transfers between devices: 135 us -> none  [reduce_blocks(): return lax.psum_scatter(grads, 'shard', scatter_dimension=0, tiled=False)]
    all_gather x1 -> x0, waiting for transfers between devices: 131 us -> none  [gather_blocks(): return lax.all_gather(mine, 'shard', axis=0, tiled=False)]
  transfers between devices with their start and end apart: 6 -> 4, of which waited for: 4 -> 2; matrix products, arithmetic and copies ran while one was open for 8% -> 7% of each run, Pallas kernels for 5% -> 49%
where the time goes in v3:
time: 466 us
  Pallas kernels  297 us (64%)
  waiting for transfers between devices  103 us (22%)
  local copies, waits for them, and re-layouts  22.2 us (5%)
  other arithmetic  16.8 us (4%)
  between operations  14.2 us (3%)
  starting transfers between devices  11.9 us (3%)
    pallas_call x1, Pallas kernels, gather_blocks(): pl.pallas_call(functools.partial(gather_kernel, shards), name='gather_blo...  129 us
    all_to_all x2, waiting for transfers between devices, exchange(): return lax.all_to_all(send, 'shard', 0, 0, tiled=True)  103 us
    pallas_call x1, Pallas kernels, reduce_blocks(): pl.pallas_call(functools.partial(reduce_kernel, shards), name='reduce_blo...  97.6 us
    pallas_call x1, Pallas kernels, local(): pl.pallas_call(functools.partial(forward_kernel, keep), name='forward_and...  45.5 us
    pallas_call x1, Pallas kernels, local(): pl.pallas_call(functools.partial(input_grad_kernel, keep), name='token_gr...  25.6 us
    all_to_all x2, starting transfers between devices, exchange(): return lax.all_to_all(send, 'shard', 0, 0, tiled=True)  11.9 us
  transfers between devices with their start and end apart: 4, of which 2 were waited for; matrix products, arithmetic and copies ran while one was open for 7% of the time, Pallas kernels for 49%

profile of v3, /device:TPU:0, one launch (start us, length us, event | category | flops | bytes accessed | tf_op | source)
XLA Modules:
  0.0 465.8 jit_solution(13457687474921782996)
XLA Ops:
  7.2 0.7 all-gather.2.cloned.1.call-update
  7.9 0.8 dynamic-slice_add_fusion
  8.9 0.2 convert_reduce_fusion
  9.1 0.2 convert_reduce_fusion.2
  9.3 0.6 dynamic_slice.15
  9.9 0.6 fusion.6
  11.2 1.3 gather_fusion.2
  12.5 0.6 compare_and_fusion.1
  13.1 2.4 gather_fusion.5
  15.5 3.3 broadcast_select_fusion
  18.8 7.5 %all-to-all-start = ((bf16[72,128,128]{2,1,0:T(8,128)(2,1)}), bf16[72,128,128]{2,1,0:T(8,128)(2,1)}, u32[]{:S(2)}, u32[]{:S(2)}) async-start(bf16[72,128,128]{2,1,0:T(8,128)(2,1)} %broadcast_select_fusion), calls=%async_computation | async-start | bytes 4718592 | tf_op jit(solution)/shard_map/all_to_all | solution.py:342
  26.4 0.8 gather_fusion
  27.3 0.8 gather_fusion.1
  28.2 0.7 reshape.440.rows_ref
  29.0 0.6 fusion.1.idx_ref.pos_ref
  29.6 50.7 %all-to-all-done = bf16[72,128,128]{2,1,0:T(8,128)(2,1)} async-done(((bf16[72,128,128]{2,1,0:T(8,128)(2,1)}), bf16[72,128,128]{2,1,0:T(8,128)(2,1)}, u32[]{:S(2)}, u32[]{:S(2)}) %all-to-all-start) | async-done | bytes 2359328 | tf_op jit(solution)/shard_map/all_to_all | solution.py:342
  80.2 2.4 gather_fusion.3
  82.7 1.2 broadcast_select_fusion.2.held_ref
  83.9 128.6 %gather_blocks.1 = bf16[8,36,128,128]{3,2,1,0:T(8,128)(2,1)} custom-call(bf16[36,128,128]{2,1,0:T(8,128)(2,1)} %broadcast_select_fusion.2.held_ref), custom_call_target="tpu_custom_call" | custom-call | tf_op jit(solution)/shard_map/gather_blocks/pallas_call | solution.py:245
  212.5 4.6 copy.23
  217.1 45.5 %forward_and_weight_grad.1 = (bf16[4,128,3072]{2,1,0:T(8,128)(2,1)}, bf16[512,3072]{1,0:T(8,128)(2,1)}, bf16[288,128,128]{2,1,0:T(8,128)(2,1)}) custom-call(s32[288]{0:T(512)} %fusion.1.idx_ref.pos_ref, s32[288]{0:T(512)} %reshape.440.rows_ref, s32[288]{0:T(512)} %fusion.1.idx_ref.pos_ref, bf16[512,3072]{1,0:T(8,128)(2,1)} %bitcast.38, ...), custom_call_target="tpu_custom_call" | custom-call | flops 19327352832 | bytes 62914560 | tf_op jit(solution)/shard_map/forward_and_weight_grad/pallas_call | solution.py:396
  262.7 25.6 %token_grad.1 = bf16[512,3072]{1,0:T(8,128)(2,1)} custom-call(s32[288]{0:T(512)} %fusion.1.idx_ref.pos_ref, s32[288]{0:T(512)} %reshape.440.rows_ref, bf16[512,3072]{1,0:T(8,128)(2,1)} %get-tuple-element.8.slope_ref, bf16[288,128,128]{2,1,0:T(8,128)(2,1)} %bitcast.36), custom_call_target="tpu_custom_call" | custom-call | flops 9663676416 | bytes 31457280 | tf_op jit(solution)/shard_map/token_grad/pallas_call | solution.py:432
  288.4 97.6 %reduce_blocks.1 = bf16[36,128,128]{2,1,0:T(8,128)(2,1)} custom-call(bf16[8,36,128,128]{3,2,1,0:T(8,128)(2,1)} %bitcast.34), custom_call_target="tpu_custom_call" | custom-call | tf_op jit(solution)/shard_map/reduce_blocks/pallas_call | solution.py:323
  386.0 3.7 gather_fusion.4
  389.7 3.3 broadcast_select_fusion.1
  393.0 4.4 all-to-all-start.1
  397.4 0.2 convert_reduce_fusion.1
  397.6 0.6 compare_and_fusion
  398.2 0.2 compare_reduce_fusion
  398.4 51.9 %all-to-all-done.1 = bf16[72,128,128]{2,1,0:T(8,128)(2,1)} async-done(((bf16[72,128,128]{2,1,0:T(8,128)(2,1)}), bf16[72,128,128]{2,1,0:T(8,128)(2,1)}, u32[]{:S(2)}, u32[]{:S(2)}) %all-to-all-start.1) | async-done | bytes 2359328 | tf_op jit(solution)/shard_map/all_to_all | solution.py:342
  450.3 4.1 gather_fusion.6
  454.3 4.6 select_bitcast_fusion
  (41 shorter events, 1.4 us)
Async XLA Ops:
  7.2 5.9 %copy-start = (bf16[1,72,128,128]{3,2,1,0:T(8,128)(2,1)S(1)}, bf16[1,72,128,128]{3,2,1,0:T(8,128)(2,1)}, u32[]{:S(2)}) copy-start(bf16[1,72,128,128]{3,2,1,0:T(8,128)(2,1)} %param.9) | copy-start | bytes 7077892
  7.2 205.3 %all-gather.2.cloned.1.call-start = ((), (), s32[]{:S(2)}) async-start(), calls=%async_computation.3 | async-start | bytes 3932160 | tf_op jit(solution)/shard_map/all_gather | solution.py:388
  18.8 9.2 %copy-start.1 = (s32[96,12]{0,1:T(8,128)S(1)}, s32[96,12]{0,1:T(8,128)}, u32[]{:S(2)}) copy-start(s32[96,12]{0,1:T(8,128)} %param.10) | copy-start | bytes 13828
  18.8 61.4 %all-to-all-start = ((bf16[72,128,128]{2,1,0:T(8,128)(2,1)}), bf16[72,128,128]{2,1,0:T(8,128)(2,1)}, u32[]{:S(2)}, u32[]{:S(2)}) async-start(bf16[72,128,128]{2,1,0:T(8,128)(2,1)} %broadcast_select_fusion), calls=%async_computation | async-start | bytes 4718592 | tf_op jit(solution)/shard_map/all_to_all | solution.py:342
  26.4 432.6 %reduce-scatter.2.cloned.1.call-start = ((), (), s32[]{:S(2)}) async-start(), calls=%async_computation.4 | async-start | bytes 3932160 | tf_op jit(solution)/shard_map/reduce_scatter | solution.py:457
  386.0 3.7 copy-start.2
  393.0 57.2 %all-to-all-start.1 = ((bf16[72,128,128]{2,1,0:T(8,128)(2,1)}), bf16[72,128,128]{2,1,0:T(8,128)(2,1)}, u32[]{:S(2)}, u32[]{:S(2)}) async-start(bf16[72,128,128]{2,1,0:T(8,128)(2,1)} %broadcast_select_fusion.1), calls=%async_computation.2 | async-start | bytes 4718592 | tf_op jit(solution)/shard_map/all_to_all | solution.py:342
Sparse Core Ops, SparseCore 0:
  9.6 31.2 all-gather.1
  288.4 38.3 reduce-scatter.1

commit v4 on v3

--- a/solution.py
+++ b/solution.py
@@ -193,7 +193,7 @@
     return ((0, SPLIT), (SPLIT, PIECES))[way]
 
 
-def gather_kernel(shards, held_ref, slab_ref, send_sem, recv_sem, own_sem):
+def gather_kernel(shards, held_ref, out_ref, slab_ref, send_sem, recv_sem, out_sem, own_sem):
     size = held_ref.shape[0] // PIECES
     me, here, ways = ring_place(shards)
     own = pltpu.make_async_copy(held_ref, slab_ref.at[me], own_sem)
@@ -208,12 +208,18 @@
             device_id={"shard": ways[way]}, device_id_type=pl.DeviceIdType.MESH,
         )
 
+    def store(source, piece):
+        at = pl.ds(piece * size, size)
+        return pltpu.make_async_copy(
+            slab_ref.at[source, at], out_ref.at[source, at], out_sem.at[source, piece])
+
     def source(way, hop):
         return ring_index(here - SIGN[way] * hop, shards)
 
     def own_piece(piece):
         for way in (NEXT, LAST):
             copy(way, me, piece).start()
+        store(me, piece).start()
 
     for_each(0, PIECES, own_piece)
     for hop in range(1, shards // 2 + 1):
@@ -233,12 +239,22 @@
                     def _(way=way):
                         copy(way, source(way, hop), piece).start()
 
+                first, last = hop_pieces(way, hop, shards)
+
+                @pl.when((piece >= first) & (piece < last))
+                def _(way=way):
+                    store(source(way, hop), piece).start()
+
         for_each(0, PIECES, relay)
+    for_each(0, PIECES, lambda piece: store(me, piece).wait())
     for hop in range(1, shards // 2 + 1):
         for way in (NEXT, LAST):
             for_each(*hop_pieces(way, hop, shards),
                      lambda piece, way=way, hop=hop:
                      copy(way, source(way, hop - 1), piece).wait_send())
+            for_each(*hop_pieces(way, hop, shards),
+                     lambda piece, way=way, hop=hop:
+                     store(source(way, hop), piece).wait())
 
 
 def gather_blocks(held, shards):
@@ -249,11 +265,14 @@
         in_specs=[pl.BlockSpec(memory_space=pl.ANY)],
         out_specs=pl.BlockSpec(memory_space=pl.ANY),
         scratch_shapes=[
+            pltpu.VMEM((shards,) + held.shape, held.dtype),
             pltpu.SemaphoreType.DMA((2, shards, PIECES)),
+            pltpu.SemaphoreType.DMA((shards, PIECES)),
             pltpu.SemaphoreType.DMA((shards, PIECES)),
             pltpu.SemaphoreType.DMA,
         ],
-        compiler_params=pltpu.CompilerParams(collective_id=0, has_side_effects=True),
+        compiler_params=pltpu.CompilerParams(
+            collective_id=0, has_side_effects=True, vmem_limit_bytes=32 * MIB),
     )(held)
 
 

time: 466 us -> 434 us (0.931)
  Pallas kernels: 297 us -> 262 us
    pallas_call x1, Pallas kernels: 129 us -> 94 us  [gather_blocks(): pl.pallas_call(functools.partial(gather_kernel, shards), name='gather_blo...]
  transfers between devices with their start and end apart: 4 -> 4, of which waited for: 2 -> 2; matrix products, arithmetic and copies ran while one was open for 7% -> 8% of each run, Pallas kernels for 49% -> 44%
where the time goes in v4:
time: 434 us; the launch traced here: 433 us
  Pallas kernels  262 us (60%)
  waiting for transfers between devices  103 us (24%)
  local copies, waits for them, and re-layouts  25.9 us (6%)
  other arithmetic  15.8 us (4%)
  between operations  14.2 us (3%)
  starting transfers between devices  12.1 us (3%)
    all_to_all x2, waiting for transfers between devices, exchange(): return lax.all_to_all(send, 'shard', 0, 0, tiled=True)  102 us
    pallas_call x1, Pallas kernels, reduce_blocks(): pl.pallas_call(functools.partial(reduce_kernel, shards), name='reduce_blo...  96.7 us
    pallas_call x1, Pallas kernels, gather_blocks(): pl.pallas_call(functools.partial(gather_kernel, shards), name='gather_blo...  94 us
    pallas_call x1, Pallas kernels, local(): pl.pallas_call(functools.partial(forward_kernel, keep), name='forward_and...  45.5 us
    pallas_call x1, Pallas kernels, local(): pl.pallas_call(functools.partial(input_grad_kernel, keep), name='token_gr...  25.5 us
    all_to_all x2, starting transfers between devices, exchange(): return lax.all_to_all(send, 'shard', 0, 0, tiled=True)  12 us
  transfers between devices with their start and end apart: 4, of which 2 were waited for; matrix products, arithmetic and copies ran while one was open for 8% of the time, Pallas kernels for 44%

profile of v4, /device:TPU:0, one launch (start us, length us, event | category | flops | bytes accessed | tf_op | source)
XLA Modules:
  0.0 432.8 jit_solution(7208730461193179087)
XLA Ops:
  7.2 0.7 all-gather.2.cloned.1.call-update
  7.9 0.8 dynamic-slice_add_fusion
  8.9 0.2 convert_reduce_fusion
  9.1 0.2 convert_reduce_fusion.2
  9.3 0.6 dynamic_slice.15
  9.9 0.6 fusion.6
  11.2 1.3 gather_fusion.2
  12.5 0.6 compare_and_fusion.1
  13.1 2.4 gather_fusion.5
  15.5 3.3 broadcast_select_fusion
  18.8 7.5 %all-to-all-start = ((bf16[72,128,128]{2,1,0:T(8,128)(2,1)}), bf16[72,128,128]{2,1,0:T(8,128)(2,1)}, u32[]{:S(2)}, u32[]{:S(2)}) async-start(bf16[72,128,128]{2,1,0:T(8,128)(2,1)} %broadcast_select_fusion), calls=%async_computation | async-start | bytes 4718592 | tf_op jit(solution)/shard_map/all_to_all | solution.py:361
  26.4 0.8 gather_fusion
  27.3 0.8 gather_fusion.1
  28.2 0.7 reshape.440.rows_ref
  29.0 0.6 fusion.1.idx_ref.pos_ref
  29.6 50.7 %all-to-all-done = bf16[72,128,128]{2,1,0:T(8,128)(2,1)} async-done(((bf16[72,128,128]{2,1,0:T(8,128)(2,1)}), bf16[72,128,128]{2,1,0:T(8,128)(2,1)}, u32[]{:S(2)}, u32[]{:S(2)}) %all-to-all-start) | async-done | bytes 2359328 | tf_op jit(solution)/shard_map/all_to_all | solution.py:361
  80.2 2.4 gather_fusion.3
  82.7 0.2 broadcast_select_fusion.2.held_ref
  82.9 94.0 %gather_blocks.1 = bf16[8,36,128,128]{3,2,1,0:T(8,128)(2,1)S(1)} custom-call(bf16[36,128,128]{2,1,0:T(8,128)(2,1)S(1)} %broadcast_select_fusion.2.held_ref), custom_call_target="tpu_custom_call" | custom-call | tf_op jit(solution)/shard_map/gather_blocks/pallas_call | solution.py:261
  176.9 3.6 copy-done.1
  180.5 4.6 %copy.23 = bf16[512,3072]{0,1:T(8,128)(2,1)} copy(bf16[512,3072]{1,0:T(8,128)(2,1)} %bitcast.37) | data formatting | bytes 6291456 | tf_op jit(solution)/shard_map/reshape | solution.py:407
  185.2 45.5 %forward_and_weight_grad.1 = (bf16[4,128,3072]{2,1,0:T(8,128)(2,1)}, bf16[512,3072]{1,0:T(8,128)(2,1)}, bf16[288,128,128]{2,1,0:T(8,128)(2,1)}) custom-call(s32[288]{0:T(512)} %fusion.1.idx_ref.pos_ref, s32[288]{0:T(512)} %reshape.440.rows_ref, s32[288]{0:T(512)} %fusion.1.idx_ref.pos_ref, bf16[512,3072]{1,0:T(8,128)(2,1)} %bitcast.38, ...), custom_call_target="tpu_custom_call" | custom-call | flops 19327352832 | bytes 62914560 | tf_op jit(solution)/shard_map/forward_and_weight_grad/pallas_call | solution.py:415
  230.7 25.5 %token_grad.1 = bf16[512,3072]{1,0:T(8,128)(2,1)} custom-call(s32[288]{0:T(512)} %fusion.1.idx_ref.pos_ref, s32[288]{0:T(512)} %reshape.440.rows_ref, bf16[512,3072]{1,0:T(8,128)(2,1)} %get-tuple-element.8.slope_ref, bf16[288,128,128]{2,1,0:T(8,128)(2,1)} %bitcast.35), custom_call_target="tpu_custom_call" | custom-call | flops 9663676416 | bytes 31457280 | tf_op jit(solution)/shard_map/token_grad/pallas_call | solution.py:451
  256.4 96.7 %reduce_blocks.1 = bf16[36,128,128]{2,1,0:T(8,128)(2,1)} custom-call(bf16[8,36,128,128]{3,2,1,0:T(8,128)(2,1)} %bitcast.36), custom_call_target="tpu_custom_call" | custom-call | tf_op jit(solution)/shard_map/reduce_blocks/pallas_call | solution.py:342
  353.1 3.7 gather_fusion.4
  356.8 3.3 broadcast_select_fusion.1
  360.1 4.5 %all-to-all-start.1 = ((bf16[72,128,128]{2,1,0:T(8,128)(2,1)}), bf16[72,128,128]{2,1,0:T(8,128)(2,1)}, u32[]{:S(2)}, u32[]{:S(2)}) async-start(bf16[72,128,128]{2,1,0:T(8,128)(2,1)} %broadcast_select_fusion.1), calls=%async_computation.2 | async-start | bytes 4718592 | tf_op jit(solution)/shard_map/all_to_all | solution.py:361
  364.8 0.6 compare_and_fusion
  365.4 0.2 compare_reduce_fusion
  365.6 51.7 %all-to-all-done.1 = bf16[72,128,128]{2,1,0:T(8,128)(2,1)} async-done(((bf16[72,128,128]{2,1,0:T(8,128)(2,1)}), bf16[72,128,128]{2,1,0:T(8,128)(2,1)}, u32[]{:S(2)}, u32[]{:S(2)}) %all-to-all-start.1) | async-done | bytes 2359328 | tf_op jit(solution)/shard_map/all_to_all | solution.py:361
  417.3 4.1 gather_fusion.6
  421.4 4.6 %select_bitcast_fusion = f32[1,72,128,128]{3,2,1,0:T(8,128)} fusion(bf16[72,128,128]{2,1,0:T(8,128)(2,1)} %gather_fusion.6, pred[72]{0:T(512)(128)(4,1)S(1)} %get-tuple-element.10, pred[72]{0:T(512)(128)(4,1)S(1)} %compare_reduce_fusion), kind=kLoop, calls=%fused_computation.7 | loop fusion | flops 4718592 | bytes 7078032 | tf_op jit(solution)/shard_map/reshape | solution.py:484
  (43 shorter events, 1.6 us)
Async XLA Ops:
  7.2 5.9 %copy-start = (bf16[1,72,128,128]{3,2,1,0:T(8,128)(2,1)S(1)}, bf16[1,72,128,128]{3,2,1,0:T(8,128)(2,1)}, u32[]{:S(2)}) copy-start(bf16[1,72,128,128]{3,2,1,0:T(8,128)(2,1)} %param.9) | copy-start | bytes 7077892
  7.2 173.3 %all-gather.2.cloned.1.call-start = ((), (), s32[]{:S(2)}) async-start(), calls=%async_computation.3 | async-start | bytes 3932160 | tf_op jit(solution)/shard_map/all_gather | solution.py:407
  18.8 9.2 %copy-start.2 = (s32[96,12]{0,1:T(8,128)S(1)}, s32[96,12]{0,1:T(8,128)}, u32[]{:S(2)}) copy-start(s32[96,12]{0,1:T(8,128)} %param.10) | copy-start | bytes 13828
  18.8 61.4 %all-to-all-start = ((bf16[72,128,128]{2,1,0:T(8,128)(2,1)}), bf16[72,128,128]{2,1,0:T(8,128)(2,1)}, u32[]{:S(2)}, u32[]{:S(2)}) async-start(bf16[72,128,128]{2,1,0:T(8,128)(2,1)} %broadcast_select_fusion), calls=%async_computation | async-start | bytes 4718592 | tf_op jit(solution)/shard_map/all_to_all | solution.py:361
  26.4 399.6 %reduce-scatter.2.cloned.1.call-start = ((), (), s32[]{:S(2)}) async-start(), calls=%async_computation.4 | async-start | bytes 3932160 | tf_op jit(solution)/shard_map/reduce_scatter | solution.py:476
  176.9 3.7 copy-start.1
  353.0 3.7 copy-start.3
  360.1 57.2 %all-to-all-start.1 = ((bf16[72,128,128]{2,1,0:T(8,128)(2,1)}), bf16[72,128,128]{2,1,0:T(8,128)(2,1)}, u32[]{:S(2)}, u32[]{:S(2)}) async-start(bf16[72,128,128]{2,1,0:T(8,128)(2,1)} %broadcast_select_fusion.1), calls=%async_computation.2 | async-start | bytes 4718592 | tf_op jit(solution)/shard_map/all_to_all | solution.py:361
Sparse Core Ops, SparseCore 0:
  9.6 31.2 all-gather.1
  256.4 38.2 reduce-scatter.1
